TPU v7x, 32 devices: a whole 2x2x4 slice. The times are simulated.
32 devices in a mesh: row: 8 (over z, x), col: 4 (over y, core).
Axes of the slice: x: 2, y: 2, z: 4, core: 2. Of those that a mesh axis runs over, the one named last changes fastest.
Arguments:
- trailing: float32 [8192, 1536], P('row', 'col'), may hold values from -6 to 6
- reflectors: float32 [8192, 256], P('row', 'col'), may hold values from -6 to 6
- factor: float32 [256, 256], replicated, as said below
- column_sums: float32 [8192, 8], P('row', 'col'), may hold values from -6 to 6
- row_sums: float32 [16, 1536], P('row', 'col'), may hold values from -6 to 6
Outputs:
- updated: float32 [8192, 1536], P('row', 'col')
- column_checks: float32 [8192, 8], P('row', 'col')
- row_checks: float32 [16, 1536], P('row', 'col')
Inputs may be any that keep to these rules, and one draw needn't show every extreme that they name: `factor`: zero below the diagonal.
All inputs are finite; a program needn't handle non-finite values.
Results may differ from a plain program's by a relative error of at most 0.000067.
Values sent between devices are 32-bit elements; how exact they have to be, the bound alone decides.
No kernel may reach another device: no remote copies, remote signals or barrier semaphores. Data moves between devices by JAX's collectives and lax.ppermute only.
A program may use at most 64 MiB of HBM per device.

v0:
```python
import jax
import jax.numpy as jnp
from jax import lax
from jax.sharding import PartitionSpec as P


def matmul(left, right):
    return jnp.dot(left, right, precision=lax.Precision.HIGHEST, preferred_element_type=jnp.float32)


def shards(trailing, reflectors, factor, column_sums, row_sums):
    panel = lax.all_gather(reflectors, "col", axis=1, tiled=True)
    columns = trailing.shape[1]
    joined = jnp.concatenate([trailing, column_sums], axis=1)
    product = matmul(panel.T, joined)
    product_main = product[:, :columns]
    product_check = product[:, columns:]
    summed_main, summed_check = lax.psum((product_main, product_check), "row")
    main_image = matmul(factor.T, summed_main)
    check_image = matmul(factor.T, summed_check)
    updated = trailing - matmul(panel, main_image)
    column_checks = column_sums - matmul(panel, check_image)
    count = trailing.shape[0]
    local = jnp.arange(count).astype(jnp.float32)
    scale = 1.0 / jnp.sqrt(jnp.float32(count))
    weights = jnp.stack([jnp.ones((count,), jnp.float32) * scale, (local + 1.0) * scale / count])
    check_coeff = matmul(weights, panel)
    row_checks = row_sums - matmul(check_coeff, main_image)
    return (updated, column_checks, row_checks)


def solution(mesh):
    placed = (P("row", "col"), P("row", "col"), P(), P("row", "col"), P("row", "col"))
    return jax.shard_map(
        shards,
        mesh=mesh,
        in_specs=placed,
        out_specs=(P("row", "col"), P("row", "col"), P("row", "col")),
        check_vma=False,
    )
```

profile of v0, /device:TPU:0, one launch (start us, length us, event | category | flops | bytes accessed | tf_op | source)
XLA Modules:
  0.0 139.2 jit_solution(17977182560160107712)
XLA Ops:
  7.2 0.0 copy-start
  7.2 0.0 all-gather.2.cloned.1.call-start
  7.2 0.7 all-gather.2.cloned.1.call-update
  7.9 0.0 all-reduce.3.cloned.1.call-start
  8.0 0.9 copy.8
  8.9 0.0 copy-start.2
  8.9 3.1 %copy.9 = f32[1024,384]{0,1:T(8,128)} copy(f32[1024,384]{1,0:T(8,128)} %param.5) | data formatting | bytes 3145728 | tf_op args[0]
  12.0 17.0 %all-gather.2.cloned.1.call-done = f32[1024,256]{0,1:T(8,128)} async-done(((f32[1024,64]{0,1:T(8,128)}), f32[1024,256]{0,1:T(8,128)}) %all-gather.2.cloned.1.call-update) | async-done | bytes 1048592 | tf_op jit(solution)/shard_map/all_gather | solution.py:12
  29.0 0.0 copy-done.2
  29.0 4.7 %fusion.4 = f32[256,386]{0,1:T(8,128)S(1)} fusion(f32[1024,256]{0,1:T(8,128)} %all-gather.2.cloned.1.call-done, f32[1024,2]{1,0:T(8,128)S(1)} %copy.8, f32[1024,384]{1,0:T(8,128)S(1)} %copy-done.2), kind=kOutput, calls=%fused_computation.5 | convolution fusion | flops 1214646272 | bytes 3024896 | tf_op jit(solution)/shard_map/dot_general | solution.py:8
  33.8 0.0 copy-start.4
  33.8 0.8 slice.8
  34.5 21.3 %psum.15 = f32[256,2]{0,1:T(2,128)S(1)} all-reduce(f32[256,2]{0,1:T(2,128)S(1)} %slice.9), channel_id=1, replica_groups=mesh['row'=8,'col'=4] {'row'}, use_global_device_ids=true, to_apply=%region_1.0 | all-reduce | flops 512 | bytes 4096 | tf_op jit(solution)/shard_map/psum | solution.py:18
  55.9 0.0 all-reduce.3.cloned.1.call-update
  55.9 0.0 copy-done.1
  55.9 0.0 copy-start.3
  55.9 0.9 fusion.8
  56.8 0.2 fusion.13
  57.1 1.2 fusion.7
  58.3 65.9 %all-reduce.3.cloned.1.call-done = f32[256,384]{0,1:T(8,128)} async-done(((f32[256,384]{0,1:T(8,128)}), f32[256,384]{0,1:T(8,128)}) %all-reduce.3.cloned.1.call-update) | async-done | bytes 393232 | tf_op jit(solution)/shard_map/psum | solution.py:18
  124.2 1.5 %fusion.12 = f32[384,256]{1,0:T(8,128)S(1)} fusion(f32[256,384]{0,1:T(8,128)} %all-reduce.3.cloned.1.call-done, f32[256,256]{1,0:T(8,128)S(1)} %copy-done), kind=kOutput, calls=%fused_computation.14 | convolution fusion | flops 301989888 | bytes 1048576 | tf_op jit(solution)/shard_map/dot_general | solution.py:8
  125.7 2.6 %bitcast_subtract_fusion = f32[1024,384]{0,1:T(8,128)} fusion(f32[1024,384]{0,1:T(8,128)S(1)} %copy-done.3, f32[384,256]{1,0:T(8,128)S(1)} %fusion.12, f32[1024,256]{0,1:T(8,128)S(1)} %copy-done.1), kind=kOutput, calls=%fused_computation.4 | convolution fusion | flops 1208352768 | bytes 4587520 | tf_op jit(solution)/shard_map/dot_general | solution.py:8
  128.3 3.0 %copy.10 = f32[1024,384]{1,0:T(8,128)} copy(f32[1024,384]{0,1:T(8,128)} %bitcast_subtract_fusion) | data formatting | bytes 3145728
  131.4 1.0 convolution_subtract_fusion
  (8 shorter events, 0.0 us)
Async XLA Ops:
  7.2 49.7 %copy-start = (f32[256,256]{1,0:T(8,128)S(1)}, f32[256,256]{1,0:T(8,128)}, u32[]{:S(2)}) copy-start(f32[256,256]{1,0:T(8,128)} %param.7) | copy-start | bytes 786436
  7.2 21.8 %all-gather.2.cloned.1.call-start = ((), (), s32[]{:S(2)}) async-start(), calls=%async_computation | async-start | bytes 1310720 | tf_op jit(solution)/shard_map/all_gather | solution.py:12
  7.9 116.3 %all-reduce.3.cloned.1.call-start = ((), (), s32[]{:S(2)}) async-start(), calls=%async_computation.1 | async-start | bytes 786432 | tf_op jit(solution)/shard_map/psum | solution.py:18
  8.9 20.1 %copy-start.2 = (f32[1024,384]{1,0:T(8,128)S(1)}, f32[1024,384]{1,0:T(8,128)}, u32[]{:S(2)}) copy-start(f32[1024,384]{1,0:T(8,128)} %param.5) | copy-start | bytes 4718596
  29.0 26.9 %copy-start.1 = (f32[1024,256]{0,1:T(8,128)S(1)}, f32[1024,256]{0,1:T(8,128)}, u32[]{:S(2)}) copy-start(f32[1024,256]{0,1:T(8,128)} %all-gather.2.cloned.1.call-done) | copy-start | bytes 3145732
  33.8 23.3 %copy-start.4 = (f32[1024,2]{0,1:T(2,128)S(1)}, f32[1024,2]{0,1:T(2,128)}, u32[]{:S(2)}) copy-start(f32[1024,2]{0,1:T(2,128)} %param.8) | copy-start | bytes 24580
  55.9 69.8 %copy-start.3 = (f32[1024,384]{0,1:T(8,128)S(1)}, f32[1024,384]{0,1:T(8,128)}, u32[]{:S(2)}) copy-start(f32[1024,384]{0,1:T(8,128)} %copy.9) | copy-start | bytes 4718596
  128.3 3.0 %copy-start.5 = (f32[2,384]{1,0:T(2,128)S(1)}, f32[2,384]{1,0:T(2,128)}, u32[]{:S(2)}) copy-start(f32[2,384]{1,0:T(2,128)} %param.9) | copy-start | bytes 9220
Sparse Core Ops, SparseCore 0:
  9.5 19.4 all-gather.1
  56.0 68.1 all-reduce.2
where the time goes:
time: 139 us
  waiting for transfers between devices  83.6 us (60%)
  blocking collectives  21.3 us (15%)
  between operations  14.1 us (10%)
  matrix products  12.2 us (9%)
  local copies, waits for them, and re-layouts  7.89 us (6%)
    psum x1, waiting for transfers between devices, shards(): summed_main, summed_check = lax.psum((product_main, product_check), 'row')  65.9 us
    psum x1, blocking collectives, shards(): summed_main, summed_check = lax.psum((product_main, product_check), 'row')  21.3 us
    all_gather x1, waiting for transfers between devices, shards(): panel = lax.all_gather(reflectors, 'col', axis=1, tiled=True)  17 us
    dot_general x7, matrix products, matmul(): jnp.dot(left, right, precision=lax.Precision.HIGHEST, preferred_element_t...  12.2 us
    unnamed x15, local copies, waits for them, and re-layouts  7.12 us
  transfers between devices with their start and end apart: 2, of which 2 were waited for; matrix products, arithmetic and copies ran while one was open for 5% of the time, Pallas kernels for 0%

commit v1 on v0

--- a/solution.py
+++ b/solution.py
@@ -9,7 +9,25 @@
 
 
 def shards(trailing, reflectors, factor, column_sums, row_sums):
-    panel = lax.all_gather(reflectors, "col", axis=1, tiled=True)
+    peers, mine, span = (lax.axis_size("col"), lax.axis_index("col"), reflectors.shape[1])
+    forward = [(i, (i + 1) % peers) for i in range(peers)]
+    backward = [(i, (i - 1) % peers) for i in range(peers)]
+    panel = jnp.zeros(
+        (*reflectors.shape[:1], peers * span, *reflectors.shape[1 + 1 :]), reflectors.dtype
+    )
+    panel = lax.dynamic_update_slice_in_dim(panel, reflectors, mine * span, axis=1)
+    from_left = from_right = reflectors
+    half = peers // 2
+    for step in range(1, half + 1):
+        from_left = lax.ppermute(from_left, "col", forward)
+        panel = lax.dynamic_update_slice_in_dim(
+            panel, from_left, (mine - step) % peers * span, axis=1
+        )
+        if step < peers - half:
+            from_right = lax.ppermute(from_right, "col", backward)
+            panel = lax.dynamic_update_slice_in_dim(
+                panel, from_right, (mine + step) % peers * span, axis=1
+            )
     columns = trailing.shape[1]
     joined = jnp.concatenate([trailing, column_sums], axis=1)
     product = matmul(panel.T, joined)

time: 139 us -> 117 us (0.84)
  waiting for transfers between devices: 83.6 us -> 54.8 us
  starting transfers between devices: 0.08 us -> 5.03 us
  blocking collectives: 21.3 us -> 23.3 us
    all_gather x1 -> x0, waiting for transfers between devices: 17 us -> none  [shards(): panel = lax.all_gather(reflectors, 'col', axis=1, tiled=True)]
    psum x1, waiting for transfers between devices: 65.9 us -> 50.1 us  [shards(): summed_main, summed_check = lax.psum((product_main, product_check), 'row')]
    unnamed x15 -> x11, local copies, waits for them, and re-layouts: 7.12 us -> 0.99 us
    ppermute x0 -> x3, starting transfers between devices: none -> 4.99 us  [the longest x2 2.98 us: shards(): from_left = lax.ppermute(from_left, 'col', forward)]
    ppermute x0 -> x3, waiting for transfers between devices: none -> 4.69 us  [the longest x2 4.68 us: shards(): from_left = lax.ppermute(from_left, 'col', forward)]
    dynamic_update_slice x0 -> x4, local copies, waits for them, and re-layouts: none -> 4.01 us  [the longest x2 1.94 us: shards(): lax.dynamic_update_slice_in_dim(panel, from_left, (mine - step) % peers *...]
    psum x1, blocking collectives: 21.3 us -> 23.3 us  [shards(): summed_main, summed_check = lax.psum((product_main, product_check), 'row')]
  transfers between devices with their start and end apart: 2 -> 4, of which waited for: 2 -> 3; matrix products, arithmetic and copies ran while one was open for 5% -> 5% of each run, Pallas kernels for 0% -> 0%
where the time goes in v1:
time: 117 us
  waiting for transfers between devices  54.8 us (47%)
  blocking collectives  23.3 us (20%)
  between operations  14.2 us (12%)
  matrix products  12.9 us (11%)
  local copies, waits for them, and re-layouts  6.58 us (6%)
  starting transfers between devices  5.03 us (4%)
    psum x1, waiting for transfers between devices, shards(): summed_main, summed_check = lax.psum((product_main, product_check), 'row')  50.1 us
    psum x1, blocking collectives, shards(): summed_main, summed_check = lax.psum((product_main, product_check), 'row')  23.3 us
    dot_general x7, matrix products, matmul(): jnp.dot(left, right, precision=lax.Precision.HIGHEST, preferred_element_t...  12.9 us
    ppermute x2, waiting for transfers between devices, shards(): from_left = lax.ppermute(from_left, 'col', forward)  4.68 us
    ppermute x2, starting transfers between devices, shards(): from_left = lax.ppermute(from_left, 'col', forward)  2.98 us
  transfers between devices with their start and end apart: 4, of which 3 were waited for; matrix products, arithmetic and copies ran while one was open for 5% of the time, Pallas kernels for 0%

profile of v1, /device:TPU:0, one launch (start us, length us, event | category | flops | bytes accessed | tf_op | source)
XLA Modules:
  0.0 116.9 jit_solution(137318740897264365)
XLA Ops:
  7.2 0.0 all-reduce.3.cloned.1.call-start
  7.2 0.5 collective-permute-start
  7.8 2.0 %collective-permute-start.1 = (f32[1024,64]{0,1:T(8,128)}, f32[1024,64]{0,1:T(8,128)}, u32[]{:S(2)}, u32[]{:S(2)}) collective-permute-start(f32[1024,64]{0,1:T(8,128)} %param.6), channel_id=1, source_target_pairs={{0,3},{1,0},{2,1},{3,2},{4,7},{5,4},{6,5},{7,6},{8,11},{9,8},{10,9... | collective-permute-start | bytes 786440 | tf_op jit(solution)/shard_map/ppermute | solution.py:27
  9.8 0.1 broadcast_in_dim.3
  9.9 1.1 constant_dynamic-update-slice_fusion.3
  11.0 3.3 %collective-permute-done = f32[1024,64]{0,1:T(8,128)} collective-permute-done((f32[1024,64]{0,1:T(8,128)}, f32[1024,64]{0,1:T(8,128)}, u32[]{:S(2)}, u32[]{:S(2)}) %collective-permute-start) | collective-permute-done | bytes 262176 | tf_op jit(solution)/shard_map/ppermute | solution.py:22
  14.3 2.4 %collective-permute-start.2 = (f32[1024,64]{0,1:T(8,128)}, f32[1024,64]{0,1:T(8,128)}, u32[]{:S(2)}, u32[]{:S(2)}) collective-permute-start(f32[1024,64]{0,1:T(8,128)} %collective-permute-done), channel_id=1, source_target_pairs={{0,1},{1,2},{2,3},{3,0},{4,5},{5,6},{6,7},{7,4},{8,9},{9,10},{10,1... | collective-permute-start | bytes 786440 | tf_op jit(solution)/shard_map/ppermute | solution.py:22
  16.8 0.2 copy.8
  17.1 1.0 constant_dynamic-update-slice_fusion.2
  18.1 1.0 constant_dynamic-update-slice_fusion.1
  19.0 1.4 %collective-permute-done.2 = f32[1024,64]{0,1:T(8,128)} collective-permute-done((f32[1024,64]{0,1:T(8,128)}, f32[1024,64]{0,1:T(8,128)}, u32[]{:S(2)}, u32[]{:S(2)}) %collective-permute-start.2) | collective-permute-done | bytes 262176 | tf_op jit(solution)/shard_map/ppermute | solution.py:22
  20.4 1.0 constant_dynamic-update-slice_fusion
  21.4 3.4 %fusion = f32[256,386]{0,1:T(8,128)S(1)} fusion(f32[1024,256]{0,1:T(8,128)S(1)} %constant_dynamic-update-slice_fusion, f32[1024,2]{1,0:T(8,128)S(1)} %copy.8, f32[1024,384]{1,0:T(8,128)S(1)} %copy-done.1), kind=kOutput, calls=%fused_computation | convolution fusion | flops 1214646272 | bytes 3024896 | tf_op jit(solution)/shard_map/dot_general | solution.py:8
  24.9 0.7 copy-done.2
  25.6 0.8 slice.8
  26.4 0.7 slice.9
  27.1 0.9 fusion.4
  28.0 23.3 %psum.15 = f32[256,2]{0,1:T(2,128)S(1)} all-reduce(f32[256,2]{0,1:T(2,128)S(1)} %slice.9), channel_id=1, replica_groups=mesh['row'=8,'col'=4] {'row'}, use_global_device_ids=true, to_apply=%region_1.2 | all-reduce | flops 512 | bytes 4096 | tf_op jit(solution)/shard_map/psum | solution.py:36
  51.3 0.2 fusion.9
  51.5 1.3 %convolution_subtract_fusion.1 = f32[1024,2]{0,1:T(2,128)} fusion(f32[1024,2]{0,1:T(2,128)S(1)} %copy-done.3, f32[1024,256]{0,1:T(8,128)S(1)} %constant_dynamic-update-slice_fusion, f32[2,256]{1,0:T(2,128)S(1)} %fusion.9), kind=kOutput, calls=%fused_computation.5 | convolution fusion | flops 6293504 | bytes 1067008 | tf_op jit(solution)/shard_map/dot_general | solution.py:8
  52.8 50.1 %all-reduce.3.cloned.1.call-done = f32[256,384]{0,1:T(8,128)} async-done(((f32[256,384]{0,1:T(8,128)}), f32[256,384]{0,1:T(8,128)}) %all-reduce.3.cloned.1.call-update) | async-done | bytes 393232 | tf_op jit(solution)/shard_map/psum | solution.py:36
  102.9 1.5 %fusion.8 = f32[384,256]{1,0:T(8,128)S(1)} fusion(f32[256,384]{0,1:T(8,128)} %all-reduce.3.cloned.1.call-done, f32[256,256]{1,0:T(8,128)S(1)} %copy-done), kind=kOutput, calls=%fused_computation.16 | convolution fusion | flops 301989888 | bytes 1048576 | tf_op jit(solution)/shard_map/dot_general | solution.py:8
  104.4 4.6 %convolution_subtract_fusion = f32[1024,384]{1,0:T(8,128)} fusion(f32[1024,384]{1,0:T(8,128)S(1)} %copy-done.1, f32[1024,256]{0,1:T(8,128)S(1)} %constant_dynamic-update-slice_fusion, f32[384,256]{1,0:T(8,128)S(1)} %fusion.8), kind=kOutput, calls=%fused_computation.4 | convolution fusion | flops 1208352768 | bytes 4587520 | tf_op jit(solution)/shard_map/dot_general | solution.py:8
  109.0 1.0 convolution_subtract_fusion.2
  (12 shorter events, 0.1 us)
Async XLA Ops:
  7.2 44.2 %copy-start = (f32[256,256]{1,0:T(8,128)S(1)}, f32[256,256]{1,0:T(8,128)}, u32[]{:S(2)}) copy-start(f32[256,256]{1,0:T(8,128)} %param.7) | copy-start | bytes 786436
  7.2 9.6 %copy-start.3 = (f32[1024,2]{0,1:T(2,128)S(1)}, f32[1024,2]{0,1:T(2,128)}, u32[]{:S(2)}) copy-start(f32[1024,2]{0,1:T(2,128)} %param.8) | copy-start | bytes 24580
  7.2 95.7 %all-reduce.3.cloned.1.call-start = ((), (), s32[]{:S(2)}) async-start(), calls=%async_computation | async-start | bytes 786432 | tf_op jit(solution)/shard_map/psum | solution.py:36
  7.2 7.1 %collective-permute-start = (f32[1024,64]{0,1:T(8,128)}, f32[1024,64]{0,1:T(8,128)}, u32[]{:S(2)}, u32[]{:S(2)}) collective-permute-start(f32[1024,64]{0,1:T(8,128)} %param.6), channel_id=1, source_target_pairs={{0,1},{1,2},{2,3},{3,0},{4,5},{5,6},{6,7},{7,4},{8,9},{9,10},{10,1... | collective-permute-start | bytes 786440 | tf_op jit(solution)/shard_map/ppermute | solution.py:22
  7.8 10.3 %collective-permute-start.1 = (f32[1024,64]{0,1:T(8,128)}, f32[1024,64]{0,1:T(8,128)}, u32[]{:S(2)}, u32[]{:S(2)}) collective-permute-start(f32[1024,64]{0,1:T(8,128)} %param.6), channel_id=1, source_target_pairs={{0,3},{1,0},{2,1},{3,2},{4,7},{5,4},{6,5},{7,6},{8,11},{9,8},{10,9... | collective-permute-start | bytes 786440 | tf_op jit(solution)/shard_map/ppermute | solution.py:27
  9.9 11.5 %copy-start.1 = (f32[1024,384]{1,0:T(8,128)S(1)}, f32[1024,384]{1,0:T(8,128)}, u32[]{:S(2)}) copy-start(f32[1024,384]{1,0:T(8,128)} %param.5) | copy-start | bytes 4718596
  14.3 6.1 %collective-permute-start.2 = (f32[1024,64]{0,1:T(8,128)}, f32[1024,64]{0,1:T(8,128)}, u32[]{:S(2)}, u32[]{:S(2)}) collective-permute-start(f32[1024,64]{0,1:T(8,128)} %collective-permute-done), channel_id=1, source_target_pairs={{0,1},{1,2},{2,3},{3,0},{4,5},{5,6},{6,7},{7,4},{8,9},{9,10},{10,1... | collective-permute-start | bytes 786440 | tf_op jit(solution)/shard_map/ppermute | solution.py:22
  24.9 0.8 copy-start.2
  104.4 4.6 %copy-start.4 = (f32[2,384]{1,0:T(2,128)S(1)}, f32[2,384]{1,0:T(2,128)}, u32[]{:S(2)}) copy-start(f32[2,384]{1,0:T(2,128)} %param.9) | copy-start | bytes 9220
Sparse Core Ops, SparseCore 0:
  27.2 75.6 all-reduce.2
